TPU v7x, 32 devices: a whole 2x2x4 slice. The times are simulated.
32 devices in a mesh: groups: 1, row: 8 (over z, y), col: 4 (over x, core).
Axes of the slice: x: 2, y: 2, z: 4, core: 2. Of those that a mesh axis runs over, the one named last changes fastest.
Arguments:
- activations: bfloat16 [1024, 16384], P('groups', ('row', 'col')), may hold values from -2.5 to 2.5
- token_ids: int32 [1024], P('groups'), may hold values from 0 to 128255
- initial: float32 [16384, 256], P(('groups', 'row', 'col')), may hold values from -6 to 6
- block_mask: int32 [128, 2], P('groups'), may hold values 0 or 1
Outputs:
- gram: float32 [8, 4, 512, 16384], P('groups', 'col', None, 'row')
- repaired: float32 [16384, 256], P(('groups', 'row', 'col'))
All inputs are finite; a program needn't handle non-finite values.
Results may differ from a plain program's by a relative error of at most 0.0003.
Values may be sent and summed in bfloat16 or wider, within the bound.
No kernel may reach another device: no remote copies, remote signals or barrier semaphores. Data moves between devices by JAX's collectives and lax.ppermute only.
A program may use at most 128 MiB of HBM per device.

v0:
```python
import math
import jax
import jax.numpy as jnp
from jax import lax
from jax.sharding import PartitionSpec as P

D = 16384
ROWS = 1024
BLOCK = 128
ITERS = 2


def shards(activations, token_ids, initial, block_mask):
    matches = (token_ids[:, None] == token_ids[None, :]).astype(jnp.float32)
    weights = 1.0 / jnp.sum(matches, axis=1)
    weighted = (activations.astype(jnp.float32) * weights[:, None]).astype(jnp.bfloat16)
    column_panel = lax.all_gather(activations, "col", axis=1, tiled=True)
    gram_tile = lax.dot_general(
        lax.all_gather(weighted, "row", axis=1, tiled=True),
        column_panel,
        (((0,), (0,)), ((), ())),
        preferred_element_type=jnp.float32,
    ) * (1.0 / ROWS)
    shard_rows = initial.shape[0]
    col_count = lax.axis_size("col")
    first_feature = (lax.axis_index("row") * col_count + lax.axis_index("col")) * shard_rows
    block_index = (first_feature + jnp.arange(shard_rows, dtype=jnp.int32)) // BLOCK
    selector = (
        block_index[:, None] == jnp.arange(block_mask.shape[0], dtype=jnp.int32)[None, :]
    ).astype(jnp.float32)
    mask_rows = jnp.dot(selector, block_mask.astype(jnp.float32), precision=lax.Precision.HIGHEST)
    mask_full = jnp.repeat(mask_rows, BLOCK, axis=1)
    step_size = ROWS / (D + 2.0 * math.sqrt(D * ROWS) + ROWS)
    current = mask_full * initial
    for iteration in range(ITERS):
        change_now = current - initial
        projected = jnp.dot(
            activations.astype(jnp.float32), change_now, precision=lax.Precision.HIGHEST
        )
        totals = lax.psum(projected, ("row", "col"))
        pulled = lax.dot_general(
            weighted.astype(jnp.float32),
            totals,
            (((0,), (0,)), ((), ())),
            precision=lax.Precision.HIGHEST,
        ) * (1.0 / ROWS)
        current = mask_full * (current - step_size * pulled)
    gram_out = gram_tile.reshape(lax.axis_size("row"), 1, shard_rows, gram_tile.shape[1])
    return (gram_out, current)


def solution(mesh):
    in_specs = (
        P("groups", ("row", "col")),
        P("groups"),
        P(("groups", "row", "col"), None),
        P("groups", None),
    )
    out_specs = (P("groups", "col", None, "row"), P(("groups", "row", "col"), None))
    return jax.shard_map(shards, mesh=mesh, in_specs=in_specs, out_specs=out_specs, check_vma=False)
```

profile of v0, /device:TPU:0, one launch (start us, length us, event | category | flops | bytes accessed | tf_op | source)
XLA Modules:
  0.0 426.7 jit_solution(2539099986985370560)
XLA Ops:
  8.0 0.0 copy-start
  8.0 0.0 copy-start.2
  8.0 0.0 all-reduce.3.cloned.1.call-start
  8.1 1.1 fusion.8
  9.2 0.6 broadcast_in_dim.2
  9.8 4.3 %convolution_bitcast_fusion.1 = f32[1024,256]{0,1:T(8,128)} fusion(bf16[1024,512]{1,0:T(8,128)(2,1)} %param.4, f32[512,256]{1,0:T(8,128)} %param.6, f32[64,8,2,128]{3,2,1,0:T(2,128)S(1)} %bitcast.25), kind=kOutput, calls=%fused_computation.4 | convolution fusion | flops 1610874880 | bytes 3145728 | tf_op jit(solution)/shard_map/dot_general | solution.py:37
  14.1 0.0 all-reduce.3.cloned.1.call-update
  14.1 0.0 all-reduce.5.cloned.1.call-start
  14.1 0.0 copy-done.2
  14.1 0.5 convert_reduce_fusion
  14.7 0.0 copy-done
  14.7 0.3 multiply_convert_fusion
  15.0 0.0 copy-start.1
  15.0 132.6 %all-reduce.3.cloned.1.call-done = f32[1024,256]{0,1:T(8,128)} async-done(((f32[1024,256]{0,1:T(8,128)}), f32[1024,256]{0,1:T(8,128)}) %all-reduce.3.cloned.1.call-update) | async-done | bytes 1048592 | tf_op jit(solution)/shard_map/psum | solution.py:40
  147.6 2.6 fusion.1
  150.3 3.9 convolution_bitcast_fusion
  154.1 0.0 all-reduce.5.cloned.1.call-update
  154.2 0.0 all-gather.5.cloned.1.call-start
  154.2 0.5 all-gather.5.cloned.1.call-update
  154.7 0.2 all-gather.3.cloned.1.call-start
  155.0 0.4 all-gather.3.cloned.1.call-update
  155.3 234.5 %all-reduce.5.cloned.1.call-done = f32[1024,256]{0,1:T(8,128)} async-done(((f32[1024,256]{0,1:T(8,128)}), f32[1024,256]{0,1:T(8,128)}) %all-reduce.5.cloned.1.call-update) | async-done | bytes 1048592 | tf_op jit(solution)/shard_map/psum | solution.py:40
  389.9 3.6 fusion.3
  393.5 25.8 %convolution_multiply_fusion = f32[4096,2048]{1,0:T(8,128)} fusion(bf16[1024,4096]{1,0:T(8,128)(2,1)} %all-gather.3.cloned.1.call-done, bf16[1024,2048]{1,0:T(8,128)(2,1)} %all-gather.5.cloned.1.call-done), kind=kOutput, calls=%fused_computation | convolution fusion | flops 17188257792 | bytes 46137344 | tf_op jit(solution)/shard_map/dot_general | solution.py:18
  (5 shorter events, 0.0 us)
Async XLA Ops:
  8.0 6.7 %copy-start = (bf16[1024,512]{1,0:T(8,128)(2,1)S(1)}, bf16[1024,512]{1,0:T(8,128)(2,1)}, u32[]{:S(2)}) copy-start(bf16[1024,512]{1,0:T(8,128)(2,1)} %param.4) | copy-start | bytes 3145732
  8.0 6.1 %copy-start.2 = (s32[1024]{0:T(1024)S(1)}, s32[1024]{0:T(1024)}, u32[]{:S(2)}) copy-start(s32[1024]{0:T(1024)} %param.5) | copy-start | bytes 12292
  8.0 139.6 %all-reduce.3.cloned.1.call-start = ((), (), s32[]{:S(2)}) async-start(), calls=%async_computation.2 | async-start | bytes 2097152 | tf_op jit(solution)/shard_map/psum | solution.py:40
  14.1 375.8 %all-reduce.5.cloned.1.call-start = ((), (), s32[]{:S(2)}) async-start(), calls=%async_computation.3 | async-start | bytes 2097152 | tf_op jit(solution)/shard_map/psum | solution.py:40
  15.0 139.7 %copy-start.1 = (bf16[1024,512]{1,0:T(8,128)(2,1)}, bf16[1024,512]{1,0:T(8,128)(2,1)S(1)}, u32[]{:S(2)}) copy-start(bf16[1024,512]{1,0:T(8,128)(2,1)S(1)} %multiply_convert_fusion) | copy-start | bytes 3145732
  154.2 239.3 %all-gather.5.cloned.1.call-start = ((), (), s32[]{:S(2)}) async-start(), calls=%async_computation.1 | async-start | bytes 5242880 | tf_op jit(solution)/shard_map/all_gather | solution.py:17
  154.7 238.7 %all-gather.3.cloned.1.call-start = ((), (), s32[]{:S(2)}) async-start(), calls=%async_computation | async-start | bytes 9437184 | tf_op jit(solution)/shard_map/all_gather | solution.py:19
Sparse Core Ops, SparseCore 0:
  14.2 133.3 all-reduce.2
  154.3 235.5 all-reduce.4
Sparse Core Ops, SparseCore 1:
  156.2 33.8 all-gather.4
  192.5 125.3 all-gather.2
where the time goes:
time: 427 us
  waiting for transfers between devices  368 us (86%)
  matrix products  41.3 us (10%)
  between operations  15.6 us (4%)
    psum x2, waiting for transfers between devices, shards(): totals = lax.psum(projected, ('row', 'col'))  367 us
    dot_general x1, matrix products, shards(): lax.dot_general(lax.all_gather(weighted, 'row', axis=1, tiled=True), colu...  25.8 us
  transfers between devices with their start and end apart: 4, of which 2 were waited for; matrix products, arithmetic and copies ran while one was open for 1% of the time, Pallas kernels for 0%

commit v1 on v0

--- a/solution.py
+++ b/solution.py
@@ -37,7 +37,7 @@
         projected = jnp.dot(
             activations.astype(jnp.float32), change_now, precision=lax.Precision.HIGHEST
         )
-        totals = lax.psum(projected, ("row", "col"))
+        totals = jnp.sum(lax.all_gather(projected, ("row", "col")), axis=0)
         pulled = lax.dot_general(
             weighted.astype(jnp.float32),
             totals,

time: 427 us -> 615 us (1.44)
  waiting for transfers between devices: 368 us -> 486 us
  local copies, waits for them, and re-layouts: 0.62 us -> 58.1 us
  other arithmetic: 0.84 us -> 18.9 us
    psum x2 -> x0, waiting for transfers between devices: 367 us -> none  [shards(): totals = lax.psum(projected, ('row', 'col'))]
    all_gather x0 -> x2, waiting for transfers between devices: none -> 364 us  [shards(): totals = jnp.sum(lax.all_gather(projected, ('row', 'col')), axis=0)]
    all_gather x1, waiting for transfers between devices: 0.01 us -> 121 us  [shards(): lax.all_gather(weighted, 'row', axis=1, tiled=True)]
    unnamed x6 -> x8, local copies, waits for them, and re-layouts: 0.02 us -> 57.5 us
    reduce_sum x0 -> x2, other arithmetic: none -> 15.1 us  [shards(): totals = jnp.sum(lax.all_gather(projected, ('row', 'col')), axis=0)]
  transfers between devices with their start and end apart: 4 -> 4, of which waited for: 2 -> 3; matrix products, arithmetic and copies ran while one was open for 1% -> 11% of each run, Pallas kernels for 0% -> 0%
where the time goes in v1:
time: 615 us; the launch traced here: 614 us
  waiting for transfers between devices  486 us (79%)
  local copies, waits for them, and re-layouts  58.1 us (9%)
  matrix products  37.3 us (6%)
  other arithmetic  18.9 us (3%)
  between operations  13.9 us (2%)
    all_gather x2, waiting for transfers between devices, shards(): totals = jnp.sum(lax.all_gather(projected, ('row', 'col')), axis=0)  364 us
    all_gather x1, waiting for transfers between devices, shards(): lax.all_gather(weighted, 'row', axis=1, tiled=True)  121 us
    unnamed x8, local copies, waits for them, and re-layouts  57.5 us
    dot_general x1, matrix products, shards(): lax.dot_general(lax.all_gather(weighted, 'row', axis=1, tiled=True), colu...  25.8 us
    reduce_sum x2, other arithmetic, shards(): totals = jnp.sum(lax.all_gather(projected, ('row', 'col')), axis=0)  15.1 us
  transfers between devices with their start and end apart: 4, of which 3 were waited for; matrix products, arithmetic and copies ran while one was open for 11% of the time, Pallas kernels for 0%

profile of v1, /device:TPU:0, one launch (start us, length us, event | category | flops | bytes accessed | tf_op | source)
XLA Modules:
  0.0 614.3 jit_solution(12399034532560028950)
XLA Ops:
  7.2 0.0 all-gather.11.cloned.1.call-start
  7.2 1.0 fusion.8
  8.2 0.6 broadcast_in_dim.2
  8.8 4.2 convolution_bitcast_fusion.1
  13.0 0.0 all-gather.11.cloned.1.call-update
  13.1 0.0 all-gather.9.cloned.1.call-start
  13.1 0.7 all-gather.9.cloned.1.call-update
  13.8 0.0 all-gather.7.cloned.1.call-start
  13.9 1.3 convert_reduce_fusion
  15.2 2.5 multiply_convert_fusion
  17.7 0.0 all-gather.7.cloned.1.call-update
  17.7 0.0 all-gather.13.cloned.1.call-start
  17.7 193.5 %all-gather.11.cloned.1.call-done = f32[32768,256]{0,1:T(8,128)} async-done(((f32[1024,256]{0,1:T(8,128)}), f32[32768,256]{0,1:T(8,128)}) %all-gather.11.cloned.1.call-update) | async-done | bytes 33554448 | tf_op jit(solution)/shard_map/all_gather | solution.py:40
  211.3 28.8 %copy.14 = f32[32,8,32,1024]{3,2,1,0:T(8,128)S(1)} copy(f32[32,8,32,1024]{3,1,2,0:T(8,128)} %bitcast.35) | data formatting | bytes 67108864
  240.1 7.5 %bitcast_reduce_fusion.1 = f32[1024,256]{0,1:T(8,128)S(1)} fusion(f32[32,8,32,1024]{3,2,1,0:T(8,128)S(1)} %copy.14), kind=kLoop, calls=%fused_computation.1 | loop fusion | flops 8126464 | bytes 34603008 | tf_op jit(solution)/shard_map/reduce_sum | solution.py:40
  247.6 1.3 fusion.1
  248.9 2.9 convolution_bitcast_fusion
  251.8 0.0 all-gather.9.cloned.1.call-done
  251.8 121.2 %all-gather.7.cloned.1.call-done = bf16[1024,4096]{1,0:T(8,128)(2,1)} async-done(((bf16[1024,512]{1,0:T(8,128)(2,1)}), bf16[1024,4096]{1,0:T(8,128)(2,1)}) %all-gather.7.cloned.1.call-update) | async-done | bytes 8388624 | tf_op jit(solution)/shard_map/all_gather | solution.py:19
  373.1 25.8 %convolution_multiply_fusion = f32[4096,2048]{1,0:T(8,128)} fusion(bf16[1024,4096]{1,0:T(8,128)(2,1)} %all-gather.7.cloned.1.call-done, bf16[1024,2048]{1,0:T(8,128)(2,1)} %all-gather.9.cloned.1.call-done), kind=kOutput, calls=%fused_computation.2 | convolution fusion | flops 17188257792 | bytes 46137344 | tf_op jit(solution)/shard_map/dot_general | solution.py:18
  398.9 170.5 %all-gather.13.cloned.1.call-done = f32[32768,256]{0,1:T(8,128)} async-done(((f32[1024,256]{0,1:T(8,128)}), f32[32768,256]{0,1:T(8,128)}) %all-gather.13.cloned.1.call-update) | async-done | bytes 33554448 | tf_op jit(solution)/shard_map/all_gather | solution.py:40
  569.4 28.8 %copy.15 = f32[32,8,32,1024]{3,2,1,0:T(8,128)S(1)} copy(f32[32,8,32,1024]{3,1,2,0:T(8,128)} %bitcast.36) | data formatting | bytes 67108864
  598.2 7.6 %bitcast_reduce_fusion = f32[1024,256]{0,1:T(8,128)S(1)} fusion(f32[32,8,32,1024]{3,2,1,0:T(8,128)S(1)} %copy.15), kind=kLoop, calls=%fused_computation | loop fusion | flops 8126464 | bytes 34603008 | tf_op jit(solution)/shard_map/reduce_sum | solution.py:40
  605.7 2.1 fusion.3
  (9 shorter events, 0.0 us)
Async XLA Ops:
  7.2 204.1 %all-gather.11.cloned.1.call-start = ((), (), s32[]{:S(2)}) async-start(), calls=%async_computation.2 | async-start | bytes 34603008 | tf_op jit(solution)/shard_map/all_gather | solution.py:40
  13.1 238.8 %all-gather.9.cloned.1.call-start = ((), (), s32[]{:S(2)}) async-start(), calls=%async_computation.1 | async-start | bytes 5242880 | tf_op jit(solution)/shard_map/all_gather | solution.py:17
  13.8 359.3 %all-gather.7.cloned.1.call-start = ((), (), s32[]{:S(2)}) async-start(), calls=%async_computation | async-start | bytes 9437184 | tf_op jit(solution)/shard_map/all_gather | solution.py:19
  17.7 551.7 %all-gather.13.cloned.1.call-start = ((), (), s32[]{:S(2)}) async-start(), calls=%async_computation.3 | async-start | bytes 34603008 | tf_op jit(solution)/shard_map/all_gather | solution.py:40
  240.0 7.5 %copy-start.1 = (bf16[1024,512]{1,0:T(8,128)(2,1)S(1)}, bf16[1024,512]{1,0:T(8,128)(2,1)}, u32[]{:S(2)}) copy-start(bf16[1024,512]{1,0:T(8,128)(2,1)} %multiply_convert_fusion) | copy-start | bytes 3145732
  240.0 7.5 %copy-start.2 = (f32[512,256]{1,0:T(8,128)S(1)}, f32[512,256]{1,0:T(8,128)}, u32[]{:S(2)}) copy-start(f32[512,256]{1,0:T(8,128)} %param.6) | copy-start | bytes 1572868
  240.1 8.8 %copy-start = (bf16[1024,512]{1,0:T(8,128)(2,1)S(1)}, bf16[1024,512]{1,0:T(8,128)(2,1)}, u32[]{:S(2)}) copy-start(bf16[1024,512]{1,0:T(8,128)(2,1)} %param.4) | copy-start | bytes 3145732
Sparse Core Ops, SparseCore 0:
  13.2 198.0 all-gather.10
  212.8 32.6 all-gather.8
  248.1 124.9 all-gather.6
  375.9 193.4 all-gather.12

commit v2 on v0

--- a/solution.py
+++ b/solution.py
@@ -37,7 +37,7 @@
         projected = jnp.dot(
             activations.astype(jnp.float32), change_now, precision=lax.Precision.HIGHEST
         )
-        totals = lax.psum(projected, ("row", "col"))
+        totals = lax.psum(lax.psum(projected, "col"), "row")
         pulled = lax.dot_general(
             weighted.astype(jnp.float32),
             totals,

time: 427 us -> 455 us (1.066)
  waiting for transfers between devices: 368 us -> 398 us
    psum x2 -> x4, waiting for transfers between devices: 367 us -> 237 us  [shards(): totals = lax.psum(lax.psum(projected, 'col'), 'row')]
    all_gather x1, waiting for transfers between devices: 0.01 us -> 127 us  [shards(): lax.all_gather(weighted, 'row', axis=1, tiled=True)]
    all_gather x1, waiting for transfers between devices: 0.01 us -> 31.9 us  [shards(): column_panel = lax.all_gather(activations, 'col', axis=1, tiled=True)]
  transfers between devices with their start and end apart: 4 -> 6, of which waited for: 2 -> 6; matrix products, arithmetic and copies ran while one was open for 1% -> 1% of each run, Pallas kernels for 0% -> 0%
where the time goes in v2:
time: 455 us
  waiting for transfers between devices  398 us (87%)
  matrix products  41.2 us (9%)
  between operations  14.2 us (3%)
    psum x4, waiting for transfers between devices, shards(): totals = lax.psum(lax.psum(projected, 'col'), 'row')  237 us
    all_gather x1, waiting for transfers between devices, shards(): lax.all_gather(weighted, 'row', axis=1, tiled=True)  127 us
    all_gather x1, waiting for transfers between devices, shards(): column_panel = lax.all_gather(activations, 'col', axis=1, tiled=True)  31.9 us
    dot_general x1, matrix products, shards(): lax.dot_general(lax.all_gather(weighted, 'row', axis=1, tiled=True), colu...  25.8 us
  transfers between devices with their start and end apart: 6, of which 6 were waited for; matrix products, arithmetic and copies ran while one was open for 1% of the time, Pallas kernels for 0%

profile of v2, /device:TPU:0, one launch (start us, length us, event | category | flops | bytes accessed | tf_op | source)
XLA Modules:
  0.0 455.0 jit_solution(9968012478435341155)
XLA Ops:
  7.2 0.0 all-reduce.5.cloned.1.call-start
  7.3 1.1 fusion.8
  8.3 0.6 broadcast_in_dim.2
  8.9 4.2 convolution_bitcast_fusion.1
  13.2 0.0 all-reduce.5.cloned.1.call-update
  13.2 0.0 all-reduce.7.cloned.1.call-start
  13.2 39.1 %all-reduce.5.cloned.1.call-done = f32[1024,256]{0,1:T(8,128)} async-done(((f32[1024,256]{0,1:T(8,128)}), f32[1024,256]{0,1:T(8,128)}) %all-reduce.5.cloned.1.call-update) | async-done | bytes 1048592 | tf_op jit(solution)/shard_map/psum | solution.py:40
  52.4 0.0 all-reduce.9.cloned.1.call-start
  52.4 0.5 convert_reduce_fusion
  53.0 0.3 multiply_convert_fusion
  53.3 81.4 %all-reduce.7.cloned.1.call-done = f32[1024,256]{0,1:T(8,128)} async-done(((f32[1024,256]{0,1:T(8,128)}), f32[1024,256]{0,1:T(8,128)}) %all-reduce.7.cloned.1.call-update) | async-done | bytes 1048592 | tf_op jit(solution)/shard_map/psum | solution.py:40
  134.7 2.6 fusion.1
  137.3 3.9 convolution_bitcast_fusion
  141.2 0.0 all-reduce.11.cloned.1.call-start
  141.3 36.0 %all-reduce.9.cloned.1.call-done = f32[1024,256]{0,1:T(8,128)} async-done(((f32[1024,256]{0,1:T(8,128)}), f32[1024,256]{0,1:T(8,128)}) %all-reduce.9.cloned.1.call-update) | async-done | bytes 1048592 | tf_op jit(solution)/shard_map/psum | solution.py:40
  177.3 0.0 all-gather.5.cloned.1.call-start
  177.3 0.5 all-gather.5.cloned.1.call-update
  177.9 0.2 all-gather.3.cloned.1.call-start
  178.1 0.3 all-gather.3.cloned.1.call-update
  178.4 81.0 %all-reduce.11.cloned.1.call-done = f32[1024,256]{0,1:T(8,128)} async-done(((f32[1024,256]{0,1:T(8,128)}), f32[1024,256]{0,1:T(8,128)}) %all-reduce.11.cloned.1.call-update) | async-done | bytes 1048592 | tf_op jit(solution)/shard_map/psum | solution.py:40
  259.4 3.6 fusion.3
  263.0 31.9 %all-gather.5.cloned.1.call-done = bf16[1024,2048]{1,0:T(8,128)(2,1)} async-done(((bf16[1024,512]{1,0:T(8,128)(2,1)}), bf16[1024,2048]{1,0:T(8,128)(2,1)}) %all-gather.5.cloned.1.call-update) | async-done | bytes 4194320 | tf_op jit(solution)/shard_map/all_gather | solution.py:17
  294.9 127.4 %all-gather.3.cloned.1.call-done = bf16[1024,4096]{1,0:T(8,128)(2,1)} async-done(((bf16[1024,512]{1,0:T(8,128)(2,1)}), bf16[1024,4096]{1,0:T(8,128)(2,1)}) %all-gather.3.cloned.1.call-update) | async-done | bytes 8388624 | tf_op jit(solution)/shard_map/all_gather | solution.py:19
  422.3 25.8 %convolution_multiply_fusion = f32[4096,2048]{1,0:T(8,128)} fusion(bf16[1024,4096]{1,0:T(8,128)(2,1)} %all-gather.3.cloned.1.call-done, bf16[1024,2048]{1,0:T(8,128)(2,1)} %all-gather.5.cloned.1.call-done), kind=kOutput, calls=%fused_computation | convolution fusion | flops 17188257792 | bytes 46137344 | tf_op jit(solution)/shard_map/dot_general | solution.py:18
  (11 shorter events, 0.1 us)
Async XLA Ops:
  7.2 45.8 %copy-start = (bf16[1024,512]{1,0:T(8,128)(2,1)S(1)}, bf16[1024,512]{1,0:T(8,128)(2,1)}, u32[]{:S(2)}) copy-start(bf16[1024,512]{1,0:T(8,128)(2,1)} %param.4) | copy-start | bytes 3145732
  7.2 45.3 %copy-start.2 = (s32[1024]{0:T(1024)S(1)}, s32[1024]{0:T(1024)}, u32[]{:S(2)}) copy-start(s32[1024]{0:T(1024)} %param.5) | copy-start | bytes 12292
  7.2 45.2 %all-reduce.5.cloned.1.call-start = ((), (), s32[]{:S(2)}) async-start(), calls=%async_computation.2 | async-start | bytes 2097152 | tf_op jit(solution)/shard_map/psum | solution.py:40
  13.2 121.5 %all-reduce.7.cloned.1.call-start = ((), (), s32[]{:S(2)}) async-start(), calls=%async_computation.3 | async-start | bytes 2097152 | tf_op jit(solution)/shard_map/psum | solution.py:40
  52.4 124.9 %all-reduce.9.cloned.1.call-start = ((), (), s32[]{:S(2)}) async-start(), calls=%async_computation.4 | async-start | bytes 2097152 | tf_op jit(solution)/shard_map/psum | solution.py:40
  53.3 124.0 %copy-start.1 = (bf16[1024,512]{1,0:T(8,128)(2,1)}, bf16[1024,512]{1,0:T(8,128)(2,1)S(1)}, u32[]{:S(2)}) copy-start(bf16[1024,512]{1,0:T(8,128)(2,1)S(1)} %multiply_convert_fusion) | copy-start | bytes 3145732
  141.2 118.2 %all-reduce.11.cloned.1.call-start = ((), (), s32[]{:S(2)}) async-start(), calls=%async_computation.5 | async-start | bytes 2097152 | tf_op jit(solution)/shard_map/psum | solution.py:40
  177.3 117.6 %all-gather.5.cloned.1.call-start = ((), (), s32[]{:S(2)}) async-start(), calls=%async_computation.1 | async-start | bytes 5242880 | tf_op jit(solution)/shard_map/all_gather | solution.py:17
  177.9 244.5 %all-gather.3.cloned.1.call-start = ((), (), s32[]{:S(2)}) async-start(), calls=%async_computation | async-start | bytes 9437184 | tf_op jit(solution)/shard_map/all_gather | solution.py:19
Sparse Core Ops, SparseCore 0:
  13.3 39.0 all-reduce.4
  55.9 78.7 all-reduce.6
  141.3 35.8 all-reduce.8
  180.6 78.7 all-reduce.10
  260.8 34.0 all-gather.4
  297.4 124.9 all-gather.2
